TPU v7x, 32 devices: a whole 2x2x4 slice. The times are simulated.
32 devices in a mesh: seq: 8 (over z, y), chan: 4 (over x, core).
Axes of the slice: x: 2, y: 2, z: 4, core: 2. Of those that a mesh axis runs over, the one named last changes fastest.
Arguments:
- features: bfloat16 [2048, 3, 8192], P(('seq', 'chan')), may hold values from -6 to 6
- cotangent: bfloat16 [2048, 8192], P('seq', 'chan'), may hold values from -6 to 6
- short_filter: float32 [3, 512, 7], P(None, 'chan'), may hold values from -2.5 to 2.5
- medium_filter: float32 [512, 128], P('chan'), may hold values from -0.5 to 0.5
- doc_start: int32 [8], replicated, may hold values from 0 to 255
Outputs:
- hyena_out: bfloat16 [2048, 8192], P('seq', 'chan')
- feature_grad: bfloat16 [2048, 3, 8192], P(('seq', 'chan'))
Inputs may be any that keep to these rules, and one draw needn't show every extreme that they name: Each shard holds exactly one document start, at position doc_start[i] of its 256 positions.
All inputs are finite; a program needn't handle non-finite values.
Results may differ from a plain program's by a relative error of at most 0.006.
Values may be sent and summed in bfloat16 or wider, within the bound.
A program may use at most 128 MiB of HBM per device.

v0:
```python
import jax
import jax.numpy as jnp
from jax import lax
from jax.sharding import PartitionSpec as P

SHORT = 7
MEDIUM = 128
band_rows = 256


def from_behind(block, axis, distance):
    devices = range(lax.axis_size(axis))
    route = [(i - distance, i) for i in devices if i - distance in devices]
    return lax.ppermute(block, axis, route)


def segment_ids(positions, doc_start, shard_rows):
    bounds = jnp.arange(doc_start.shape[0], dtype=jnp.int32) * shard_rows + doc_start
    return jnp.sum((bounds[None, :] <= positions[:, None]).astype(jnp.int32), axis=1)


def short_forward(source, seg_ids, taps_full):
    row_count = source.shape[1] - (SHORT - 1)
    running = jnp.zeros((source.shape[0], row_count, source.shape[2]), jnp.float32)
    for offset in range(SHORT):
        row_start = SHORT - 1 - offset
        shifted = source[:, row_start : row_start + row_count]
        open_tap = seg_ids[row_start : row_start + row_count] == seg_ids[SHORT - 1 :]
        running = running + jnp.where(
            open_tap[None, :, None], taps_full[:, offset, :][:, None, :] * shifted, 0.0
        )
    return running


def short_backward(grad_short, seg_ids, taps_full):
    row_count = grad_short.shape[1]
    out_rows = row_count + SHORT - 1
    grad_padded = jnp.pad(grad_short, ((0, 0), (SHORT - 1, SHORT - 1), (0, 0)))
    seg_padded = jnp.concatenate([seg_ids, jnp.full((SHORT - 1,), -1, jnp.int32)])
    running = jnp.zeros((grad_short.shape[0], out_rows, grad_short.shape[2]), jnp.float32)
    for offset in range(SHORT):
        shifted = grad_padded[:, offset : offset + out_rows]
        open_tap = seg_ids == seg_padded[offset : offset + out_rows]
        running = running + jnp.where(
            open_tap[None, :, None], taps_full[:, offset, :][:, None, :] * shifted, 0.0
        )
    return running


def band_mats(filters_bf, seg_ids):
    lag_steps = (
        jnp.arange(band_rows, dtype=jnp.int32)[:, None]
        + MEDIUM
        - jnp.arange(band_rows + MEDIUM, dtype=jnp.int32)[None, :]
    )
    inside = (lag_steps >= 0) & (lag_steps < MEDIUM)
    lag_table = jnp.where(
        inside[None],
        jnp.take(filters_bf, jnp.clip(lag_steps, 0, MEDIUM - 1), axis=1),
        jnp.zeros((), filters_bf.dtype),
    )
    target_ids = seg_ids[MEDIUM : band_rows + MEDIUM]
    same_doc = target_ids[:, None] == seg_ids[None, :]
    matrices = [jnp.where(same_doc[None], lag_table, jnp.zeros((), lag_table.dtype))]
    return jnp.stack(matrices)


def body(features, cotangent, short_filter, medium_filter, doc_start):
    regrouped = lax.all_to_all(
        jnp.transpose(features, (1, 0, 2)), "chan", split_axis=2, concat_axis=1, tiled=True
    )
    shard_rows = regrouped.shape[1]
    local_width = regrouped.shape[2]
    local_groups = short_filter.shape[1]
    group_width = local_width // local_groups
    rim_reach = MEDIUM + SHORT - 1
    row_base = lax.axis_index("seq") * shard_rows
    positions = row_base - rim_reach + jnp.arange(shard_rows + rim_reach, dtype=jnp.int32)
    seg_all = segment_ids(positions, doc_start, shard_rows)
    taps_full = jnp.repeat(jnp.transpose(short_filter, (0, 2, 1)), group_width, axis=2)
    filters_bf = medium_filter.astype(jnp.bfloat16)
    before = from_behind(regrouped[:, shard_rows - rim_reach :], "seq", 1)
    extended = jnp.concatenate([before, regrouped], axis=1)
    short_ext = short_forward(extended, seg_all, taps_full)
    gated_ext = (short_ext[1] * short_ext[2]).astype(jnp.bfloat16)
    short_own = short_ext[:, MEDIUM:]
    blocks = shard_rows // band_rows
    window_rows = band_rows + MEDIUM
    matrices = band_mats(filters_bf, seg_all[SHORT - 1 :])
    windows = jnp.stack([gated_ext])
    windows = jnp.transpose(
        windows.reshape(blocks, window_rows, local_groups, group_width), (0, 2, 3, 1)
    )
    long_chan = jnp.einsum("bgts,bgcs->bgct", matrices, windows, preferred_element_type=jnp.float32)
    long_conv = jnp.transpose(long_chan, (0, 3, 1, 2)).reshape(shard_rows, local_width)
    query_short = short_own[0]
    key_short = short_own[1]
    value_short = short_own[2]
    hyena_out = (query_short * long_conv).astype(jnp.bfloat16)
    grad_query = cotangent * long_conv
    grad_long = (cotangent * query_short).astype(jnp.bfloat16)
    long_blocks = jnp.transpose(
        grad_long.reshape(blocks, band_rows, local_groups, group_width), (0, 2, 3, 1)
    )
    spread = jnp.einsum(
        "bgts,bgct->bgcs", matrices, long_blocks, preferred_element_type=jnp.float32
    )
    spread = jnp.transpose(spread, (0, 3, 1, 2)).reshape(blocks, window_rows, local_width)
    gated_grad = jnp.zeros((shard_rows + MEDIUM, local_width), jnp.float32)
    gated_grad = gated_grad.at[0:window_rows].add(spread[0])
    own_grad = gated_grad[MEDIUM:]
    seg_back = seg_all[MEDIUM:]
    head_grad = jnp.stack(
        [
            grad_query[: SHORT - 1],
            own_grad[: SHORT - 1] * value_short[: SHORT - 1],
            own_grad[: SHORT - 1] * key_short[: SHORT - 1],
        ],
        axis=0,
    )
    head_spread = short_backward(head_grad, seg_back[: 2 * (SHORT - 1)], taps_full)
    backward_out = jnp.concatenate(
        [gated_grad[:MEDIUM], head_spread[:, : SHORT - 1].reshape(3 * (SHORT - 1), local_width)],
        axis=0,
    )
    backward_in = from_behind(backward_out, "seq", -1)
    own_grad = own_grad.at[shard_rows - MEDIUM :].add(backward_in[:MEDIUM])
    grad_short = jnp.stack([grad_query, own_grad * value_short, own_grad * key_short], axis=0)
    spread_short = short_backward(grad_short, seg_back, taps_full)
    feature_full = (
        spread_short[:, SHORT - 1 :]
        .at[:, shard_rows - SHORT + 1 :]
        .add(backward_in[MEDIUM:].reshape(3, SHORT - 1, local_width))
    )
    restored = lax.all_to_all(
        feature_full.astype(jnp.bfloat16), "chan", split_axis=1, concat_axis=2, tiled=True
    )
    return (hyena_out, jnp.transpose(restored, (1, 0, 2)))


def solution(mesh):
    in_specs = (
        P(("seq", "chan"), None, None),
        P("seq", "chan"),
        P(None, "chan", None),
        P("chan", None),
        P(),
    )
    out_specs = (P("seq", "chan"), P(("seq", "chan"), None, None))
    return jax.shard_map(body, mesh=mesh, in_specs=in_specs, out_specs=out_specs, check_vma=False)
```

profile of v0, /device:TPU:0, one launch (start us, length us, event | category | flops | bytes accessed | tf_op | source)
XLA Modules:
  0.0 708.3 jit_solution(11230173101609217157)
XLA Ops:
  0.6 11.3 %copy.69 = bf16[64,3,8192]{0,1,2:T(4,128)(2,1)} copy(bf16[64,3,8192]{2,0,1:T(8,128)(2,1)} %param.13) | data formatting | bytes 6291456 | tf_op args[0]
  11.9 8.2 %bitcast_bitcast_fusion = bf16[8192,3,64]{2,1,0:T(4,128)(2,1)} fusion(bf16[64,3,8192]{0,1,2:T(4,128)(2,1)} %copy.69), kind=kLoop, calls=%fused_computation.145 | loop fusion | bytes 6291456
  20.1 8.6 %reshape.297 = bf16[4,2,196608]{2,1,0:T(2,128)(2,1)} reshape(bf16[8192,3,64]{2,1,0:T(4,128)(2,1)} %bitcast_bitcast_fusion) | data formatting | bytes 6291456
  28.7 4.2 all-to-all-start
  34.2 1.6 broadcast_in_dim.198
  35.7 2.1 reshape.280
  41.4 28.5 %all-to-all-done = bf16[4,2,196608]{2,1,0:T(2,128)(2,1)S(1)} async-done(((bf16[4,2,196608]{2,1,0:T(2,128)(2,1)}), bf16[4,2,196608]{2,1,0:T(2,128)(2,1)S(1)}, u32[]{:S(2)}, u32[]{:S(2)}) %all-to-all-start) | async-done | bytes 3145760 | tf_op jit(solution)/shard_map/all_to_all | solution.py:69
  69.9 6.4 reshape.298
  76.4 10.7 %copy.71 = bf16[3,4,64,2048]{3,2,1,0:T(8,128)(2,1)S(1)} copy(bf16[3,4,64,2048]{2,0,3,1:T(4,128)(2,1)} %bitcast.101) | data formatting | bytes 6291456 | tf_op jit(solution)/shard_map/all_to_all | solution.py:69
  87.0 1.6 slice.375
  88.6 5.4 collective-permute-start
  95.0 372.4 %gather_fusion = bf16[98304,128]{1,0:T(8,128)(2,1)} fusion(bf16[128,128]{0,1:T(8,128)(2,1)S(1)} %copy.73, s32[98304]{0:T(1024)} %broadcast_clamp_fusion), kind=kCustom, calls=%fused_computation | custom fusion | bytes 50724864 | tf_op jit(solution)/shard_map/jit(_take)/gather | solution.py:59
  467.4 32.0 %copy.74 = bf16[256,384,128]{1,0,2:T(8,128)(2,1)} copy(bf16[256,384,128]{2,1,0:T(8,128)(2,1)} %bitcast.100) | data formatting | bytes 50331648 | tf_op jit(solution)/shard_map/jit(_take)/gather | solution.py:59
  500.7 44.8 %select_add_fusion = f32[3,384,2048]{2,1,0:T(8,128)S(1)} fusion(bf16[3,256,2048]{2,1,0:T(8,128)(2,1)S(1)} %bitcast.103, bf16[3,134,2048]{2,1,0:T(8,128)(2,1)} %collective-permute-done, f32[3,2048]{1,0:T(4,128)S(1)} %get-tuple-element.91, f32[3,2048]{1,0:T(4,128)S(1)} %get-tuple-element.92, f32[3,2048]{1,0:T(4,128)S(1)} %get-tuple-element.93, ...), kind=kLoop, calls=%fused_computation.18 | loop fusion | flops 110886912 | bytes 14403840 | tf_op jit(solution)/shard_map/add | solution.py:29
  545.5 3.5 copy-done
  550.4 12.9 %fusion.2 = f32[128,16,256]{2,1,0:T(8,128)} fusion(bf16[128,16,384]{2,1,0:T(8,128)(2,1)S(1)} %bitcast.112, bf16[256,384,128]{1,0,2:T(8,128)(2,1)} %copy.74, pred[256,384]{1,0:T(8,128)(4,1)} %get-tuple-element.97, pred[256,384]{1,0:T(8,128)(4,1)} %get-tuple-element.84, pred[256,384]{1,0:T(8,128)(4,1)S(1)} %get-tuple-element.83), kind=kOutput, calls=%fused_computation.3 | convolution fusion | flops 440401920 | bytes 29130752 | tf_op jit(solution)/shard_map/bgts,bgcs->bgct/dot_general | solution.py:94
  563.3 1.9 copy.75
  565.2 3.8 convert_multiply_fusion.1
  570.5 16.5 %fusion.33 = f32[1,384,128,16]{1,3,2,0:T(8,128)} fusion(bf16[128,16,256]{2,1,0:T(8,128)(2,1)} %bitcast.113, bf16[256,384,128]{1,0,2:T(8,128)(2,1)} %copy.74, pred[256,384]{1,0:T(8,128)(4,1)S(1)} %get-tuple-element.83, pred[256,384]{1,0:T(8,128)(4,1)} %get-tuple-element.84, pred[256,384]{1,0:T(8,128)(4,1)} %get-tuple-element.97), kind=kOutput, calls=%fused_computation.67 | convolution fusion | flops 440401920 | bytes 29655040 | tf_op jit(solution)/shard_map/bgts,bgct->bgcs/dot_general | solution.py:105
  587.0 3.1 fusion.58
  593.6 1.6 copy.80
  597.6 3.1 slice.397
  600.8 3.1 copy.82
  605.4 21.7 %collective-permute-done.1 = f32[146,2048]{1,0:T(8,128)} collective-permute-done((f32[146,2048]{1,0:T(8,128)}, f32[146,2048]{1,0:T(8,128)}, u32[]{:S(2)}, u32[]{:S(2)}) %collective-permute-start.1) | collective-permute-done | bytes 1196064 | tf_op jit(solution)/shard_map/ppermute | solution.py:14
  627.1 2.3 fusion.36
  629.4 5.4 fusion.32
  636.3 8.0 %fusion.10 = f32[3,262,2048]{2,1,0:T(8,128)S(1)} fusion(f32[3,268,2048]{2,1,0:T(8,128)S(1)} %select_maximum_fusion, f32[3,2048]{1,0:T(4,128)S(1)} %get-tuple-element.91, f32[3,2048]{1,0:T(4,128)S(1)} %get-tuple-element.92, f32[3,2048]{1,0:T(4,128)S(1)} %get-tuple-element.93, f32[3,2048]{1,0:T(4,128)S(1)} %copy-done.4, f32[3,2048]{1,0:T(4,128)S(1)} %get-tuple-element.95, ...), kind=kLoop, calls=%fused_computation.24 | loop fusion | flops 30584832 | bytes 51684900 | tf_op jit(solution)/shard_map/add | solution.py:44
  644.4 2.7 copy-done.1
  650.3 2.7 copy.83
  653.0 50.7 %all_to_all.36 = bf16[3,256,2048]{2,0,1:T(4,128)(2,1)S(1)} all-to-all(bf16[3,256,2048]{2,0,1:T(4,128)(2,1)S(1)} %copy.83), channel_id=1, replica_groups=mesh['seq'=8,'chan'=4] {'chan'}, dimensions={1} | all-to-all | bytes 6291456 | tf_op jit(solution)/shard_map/all_to_all | solution.py:135
  703.7 2.3 copy.84
  706.0 2.1 copy.95
  (95 shorter events, 21.6 us)
Async XLA Ops:
  20.0 12.9 %copy-start.26 = (s32[8]{0:T(128)S(1)}, s32[8]{0:T(128)}, u32[]{:S(2)}) copy-start(s32[8]{0:T(128)} %param.17) | copy-start | bytes 100
  20.1 14.1 %copy-start.15 = (f32[3,128,7]{1,2,0:T(8,128)S(1)}, f32[3,128,7]{1,2,0:T(8,128)}, u32[]{:S(2)}) copy-start(f32[3,128,7]{1,2,0:T(8,128)} %param.15) | copy-start | bytes 32260
  28.7 41.2 %all-to-all-start = ((bf16[4,2,196608]{2,1,0:T(2,128)(2,1)}), bf16[4,2,196608]{2,1,0:T(2,128)(2,1)S(1)}, u32[]{:S(2)}, u32[]{:S(2)}) async-start(bf16[4,2,196608]{2,1,0:T(2,128)(2,1)} %reshape.297), calls=%async_computation | async-start | bytes 6291456 | tf_op jit(solution)/shard_map/all_to_all | solution.py:69
  33.0 61.8 %copy-start.5 = (s32[390]{0:T(512)}, s32[390]{0:T(512)S(1)}, u32[]{:S(2)}) copy-start(s32[390]{0:T(512)S(1)} %convert_reduce_fusion) | copy-start | bytes 4684
  76.3 17.7 %copy-start.25 = (s32[12]{0:T(128)S(1)}, s32[12]{0:T(128)}, u32[]{:S(2)}) copy-start(s32[12]{0:T(128)} %slice.338) | copy-start | bytes 148
  76.3 18.5 %copy-start.13 = (f32[3,1,2048]{2,1,0:T(1,128)S(1)}, f32[3,1,2048]{2,1,0:T(1,128)}, u32[]{:S(2)}) copy-start(f32[3,1,2048]{2,1,0:T(1,128)} %get-tuple-element.64) | copy-start | bytes 73732
  76.4 18.5 %copy-start.14 = (f32[128,128]{1,0:T(8,128)S(1)}, f32[128,128]{1,0:T(8,128)}, u32[]{:S(2)}) copy-start(f32[128,128]{1,0:T(8,128)} %param.16) | copy-start | bytes 196612
  88.6 412.0 %collective-permute-start = (bf16[3,134,2048]{2,1,0:T(8,128)(2,1)}, bf16[3,134,2048]{2,1,0:T(8,128)(2,1)}, u32[]{:S(2)}, u32[]{:S(2)}) collective-permute-start(bf16[3,134,2048]{2,1,0:T(8,128)(2,1)} %slice.375), channel_id=1, source_target_pairs={{0,4},{4,8},{8,12},{12,16},{16,20},{20,24},{24,28},{1,5},{5,9},{9,... | collective-permute-start | bytes 4939784 | tf_op jit(solution)/shard_map/ppermute | solution.py:14
  467.4 33.1 %copy-start.11 = (f32[3,1,2048]{2,1,0:T(1,128)S(1)}, f32[3,1,2048]{2,1,0:T(1,128)}, u32[]{:S(2)}) copy-start(f32[3,1,2048]{2,1,0:T(1,128)} %get-tuple-element.65) | copy-start | bytes 73732
  467.4 33.1 %copy-start.12 = (f32[3,1,2048]{2,1,0:T(1,128)S(1)}, f32[3,1,2048]{2,1,0:T(1,128)}, u32[]{:S(2)}) copy-start(f32[3,1,2048]{2,1,0:T(1,128)} %get-tuple-element.66) | copy-start | bytes 73732
  467.4 33.1 %copy-start.9 = (f32[3,1,2048]{2,1,0:T(1,128)S(1)}, f32[3,1,2048]{2,1,0:T(1,128)}, u32[]{:S(2)}) copy-start(f32[3,1,2048]{2,1,0:T(1,128)} %get-tuple-element.67) | copy-start | bytes 73732
  467.4 33.2 %copy-start.10 = (f32[3,1,2048]{2,1,0:T(1,128)S(1)}, f32[3,1,2048]{2,1,0:T(1,128)}, u32[]{:S(2)}) copy-start(f32[3,1,2048]{2,1,0:T(1,128)} %get-tuple-element.68) | copy-start | bytes 73732
  467.4 33.2 %copy-start.7 = (f32[3,1,2048]{2,1,0:T(1,128)S(1)}, f32[3,1,2048]{2,1,0:T(1,128)}, u32[]{:S(2)}) copy-start(f32[3,1,2048]{2,1,0:T(1,128)} %get-tuple-element.69) | copy-start | bytes 73732
  467.4 33.2 %copy-start.8 = (f32[3,1,2048]{2,1,0:T(1,128)S(1)}, f32[3,1,2048]{2,1,0:T(1,128)}, u32[]{:S(2)}) copy-start(f32[3,1,2048]{2,1,0:T(1,128)} %get-tuple-element.70) | copy-start | bytes 73732
  467.4 33.2 %copy-start.22 = (pred[384]{0:T(512)(128)(4,1)S(1)}, pred[384]{0:T(512)(128)(4,1)}, u32[]{:S(2)}) copy-start(pred[384]{0:T(512)(128)(4,1)} %get-tuple-element.79) | copy-start | bytes 1156
  467.4 33.2 %copy-start.23 = (pred[384]{0:T(512)(128)(4,1)S(1)}, pred[384]{0:T(512)(128)(4,1)}, u32[]{:S(2)}) copy-start(pred[384]{0:T(512)(128)(4,1)} %get-tuple-element.80) | copy-start | bytes 1156
  467.4 33.2 %copy-start.24 = (pred[384]{0:T(512)(128)(4,1)S(1)}, pred[384]{0:T(512)(128)(4,1)}, u32[]{:S(2)}) copy-start(pred[384]{0:T(512)(128)(4,1)} %get-tuple-element.81) | copy-start | bytes 1156
  500.6 92.7 %copy-start.3 = (f32[3,2048]{1,0:T(4,128)}, f32[3,2048]{1,0:T(4,128)S(1)}, u32[]{:S(2)}) copy-start(f32[3,2048]{1,0:T(4,128)S(1)} %get-tuple-element.94) | copy-start | bytes 73732
  545.5 3.5 copy-start
  586.9 3.1 slice-start
  586.9 5.9 copy-start.21
  586.9 6.3 copy-start.16
  586.9 6.3 copy-start.17
  587.0 6.3 copy-start.18
  587.0 6.3 copy-start.19
  587.0 6.3 copy-start.20
  592.8 4.7 copy-start.6
  596.2 30.8 %collective-permute-start.1 = (f32[146,2048]{1,0:T(8,128)}, f32[146,2048]{1,0:T(8,128)}, u32[]{:S(2)}, u32[]{:S(2)}) collective-permute-start(f32[146,2048]{1,0:T(8,128)} %pad_maximum_fusion.1), channel_id=1, source_target_pairs={{4,0},{8,4},{12,8},{16,12},{20,16},{24,20},{28,24},{5,1},{9,5},{13... | collective-permute-start | bytes 3588104 | tf_op jit(solution)/shard_map/ppermute | solution.py:14
  629.4 5.4 copy-start.2
  634.8 1.5 copy-start.4
  644.4 2.7 copy-start.1
where the time goes:
time: 722 us; the launch traced here: 708 us
  local copies, waits for them, and re-layouts  492 us (68%)
  other arithmetic  74.1 us (10%)
  blocking collectives  50.7 us (7%)
  waiting for transfers between devices  50.2 us (7%)
  matrix products  29.4 us (4%)
  starting transfers between devices  10.9 us (2%)
    gather x2, local copies, waits for them, and re-layouts, band_mats(): jnp.take(filters_bf, jnp.clip(lag_steps, 0, MEDIUM - 1), axis=1)  404 us
    all_to_all x1, blocking collectives, body(): lax.all_to_all(feature_full.astype(jnp.bfloat16), 'chan', split_axis=1, c...  50.7 us
    add x1, other arithmetic, short_forward(): running + jnp.where(open_tap[None, :, None], taps_full[:, offset, :][:, N...  44.8 us
    unnamed x63, local copies, waits for them, and re-layouts  41.1 us
    all_to_all x1, waiting for transfers between devices, body(): lax.all_to_all(jnp.transpose(features, (1, 0, 2)), 'chan', split_axis=2,...  28.5 us
    ppermute x2, waiting for transfers between devices, from_behind(): return lax.ppermute(block, axis, route)  21.7 us
    dot_general x1, matrix products, body(): jnp.einsum('bgts,bgct->bgcs', matrices, long_blocks, preferred_element_ty...  16.5 us
  transfers between devices with their start and end apart: 3, of which 2 were waited for; matrix products, arithmetic and copies ran while one was open for 60% of the time, Pallas kernels for 0%

commit v1 on v0

--- a/solution.py
+++ b/solution.py
@@ -66,8 +66,14 @@
 
 
 def body(features, cotangent, short_filter, medium_filter, doc_start):
-    regrouped = lax.all_to_all(
-        jnp.transpose(features, (1, 0, 2)), "chan", split_axis=2, concat_axis=1, tiled=True
+    regrouped = jnp.concatenate(
+        lax.all_to_all(
+            jnp.stack(jnp.split(jnp.transpose(features, (1, 0, 2)), lax.axis_size("chan"), axis=2)),
+            "chan",
+            0,
+            0,
+        ),
+        axis=1,
     )
     shard_rows = regrouped.shape[1]
     local_width = regrouped.shape[2]

time: 722 us -> 678 us (0.939)
  local copies, waits for them, and re-layouts: 492 us -> 445 us
    unnamed x63 -> x37, local copies, waits for them, and re-layouts: 41.1 us -> 6.55 us
    all_to_all x1, local copies, waits for them, and re-layouts: 10.7 us -> 2.11 us  [body(): lax.all_to_all(jnp.stack(jnp.split(jnp.transpose(features, (1, 0, 2)), la...]
  transfers between devices with their start and end apart: 3 -> 3, of which waited for: 2 -> 2; matrix products, arithmetic and copies ran while one was open for 60% -> 62% of each run, Pallas kernels for 0% -> 0%
where the time goes in v1:
time: 678 us; the launch traced here: 670 us
  local copies, waits for them, and re-layouts  445 us (66%)
  other arithmetic  75.6 us (11%)
  waiting for transfers between devices  56.3 us (8%)
  blocking collectives  50.7 us (7%)
  matrix products  29.3 us (4%)
  starting transfers between devices  11.4 us (2%)
    gather x2, local copies, waits for them, and re-layouts, band_mats(): jnp.take(filters_bf, jnp.clip(lag_steps, 0, MEDIUM - 1), axis=1)  404 us
    all_to_all x1, blocking collectives, body(): lax.all_to_all(feature_full.astype(jnp.bfloat16), 'chan', split_axis=1, c...  50.7 us
    add x1, other arithmetic, short_forward(): running + jnp.where(open_tap[None, :, None], taps_full[:, offset, :][:, N...  45.1 us
    all_to_all x1, waiting for transfers between devices, body(): lax.all_to_all(jnp.stack(jnp.split(jnp.transpose(features, (1, 0, 2)), la...  34.4 us
    ppermute x2, waiting for transfers between devices, from_behind(): return lax.ppermute(block, axis, route)  21.9 us
    dot_general x1, matrix products, body(): jnp.einsum('bgts,bgct->bgcs', matrices, long_blocks, preferred_element_ty...  16.5 us
  transfers between devices with their start and end apart: 3, of which 2 were waited for; matrix products, arithmetic and copies ran while one was open for 62% of the time, Pallas kernels for 0%

profile of v1, /device:TPU:0, one launch (start us, length us, event | category | flops | bytes accessed | tf_op | source)
XLA Modules:
  0.0 669.7 jit_solution(9376648761500305445)
XLA Ops:
  0.6 2.1 slice_bitcast_fusion.6
  2.7 1.9 pad_maximum_fusion.1
  4.6 4.7 all-to-all-start
  12.5 34.4 %all-to-all-done = bf16[4,3,64,2048]{3,2,1,0:T(8,128)(2,1)} async-done(((bf16[4,3,64,2048]{3,2,1,0:T(8,128)(2,1)}), bf16[4,3,64,2048]{3,2,1,0:T(8,128)(2,1)}, u32[]{:S(2)}, u32[]{:S(2)}) %all-to-all-start) | async-done | bytes 3145760 | tf_op jit(solution)/shard_map/all_to_all | solution.py:70
  46.9 2.1 copy.72
  49.0 1.6 slice.375
  50.5 5.5 collective-permute-start
  57.0 372.0 %gather_fusion = bf16[98304,128]{1,0:T(8,128)(2,1)} fusion(bf16[128,128]{0,1:T(8,128)(2,1)S(1)} %copy.74, s32[98304]{0:T(1024)} %broadcast_clamp_fusion), kind=kCustom, calls=%fused_computation | custom fusion | bytes 50724864 | tf_op jit(solution)/shard_map/jit(_take)/gather | solution.py:59
  429.0 32.2 %copy.75 = bf16[256,384,128]{1,0,2:T(8,128)(2,1)} copy(bf16[256,384,128]{2,1,0:T(8,128)(2,1)} %bitcast.102) | data formatting | bytes 50331648 | tf_op jit(solution)/shard_map/jit(_take)/gather | solution.py:59
  462.3 45.1 %select_add_fusion = f32[3,384,2048]{2,1,0:T(8,128)S(1)} fusion(bf16[3,256,2048]{2,1,0:T(8,128)(2,1)S(1)} %bitcast.104, bf16[3,134,2048]{2,1,0:T(8,128)(2,1)} %collective-permute-done, f32[3,2048]{1,0:T(4,128)S(1)} %get-tuple-element.95, f32[3,2048]{1,0:T(4,128)S(1)} %get-tuple-element.96, f32[3,2048]{1,0:T(4,128)S(1)} %get-tuple-element.97, ...), kind=kLoop, calls=%fused_computation.18 | loop fusion | flops 110886912 | bytes 14403840 | tf_op jit(solution)/shard_map/add | solution.py:29
  507.4 3.6 copy-done
  512.3 12.8 %fusion.2 = f32[128,16,256]{2,1,0:T(8,128)} fusion(bf16[128,16,384]{2,1,0:T(8,128)(2,1)S(1)} %bitcast.114, bf16[256,384,128]{1,0,2:T(8,128)(2,1)} %copy.75, pred[256,384]{1,0:T(8,128)(4,1)} %get-tuple-element.101, pred[256,384]{1,0:T(8,128)(4,1)} %get-tuple-element.88, pred[256,384]{1,0:T(8,128)(4,1)S(1)} %get-tuple-element.87), kind=kOutput, calls=%fused_computation.3 | convolution fusion | flops 440401920 | bytes 29130752 | tf_op jit(solution)/shard_map/bgts,bgcs->bgct/dot_general | solution.py:100
  525.1 1.9 copy.76
  527.0 3.7 convert_multiply_fusion.1
  530.8 1.3 copy.78
  532.1 16.5 %fusion.33 = f32[1,384,128,16]{1,3,2,0:T(8,128)} fusion(bf16[128,16,256]{2,1,0:T(8,128)(2,1)} %bitcast.115, bf16[256,384,128]{1,0,2:T(8,128)(2,1)} %copy.75, pred[256,384]{1,0:T(8,128)(4,1)S(1)} %get-tuple-element.87, pred[256,384]{1,0:T(8,128)(4,1)} %get-tuple-element.88, pred[256,384]{1,0:T(8,128)(4,1)} %get-tuple-element.101), kind=kOutput, calls=%fused_computation.68 | convolution fusion | flops 440401920 | bytes 29655040 | tf_op jit(solution)/shard_map/bgts,bgct->bgcs/dot_general | solution.py:111
  548.6 3.1 fusion.58
  555.2 1.6 copy.81
  557.9 1.3 collective-permute-start.1
  559.3 3.1 slice.397
  562.4 2.9 copy.83
  565.3 1.6 copy.82
  566.9 21.9 %collective-permute-done.1 = f32[146,2048]{1,0:T(8,128)} collective-permute-done((f32[146,2048]{1,0:T(8,128)}, f32[146,2048]{1,0:T(8,128)}, u32[]{:S(2)}, u32[]{:S(2)}) %collective-permute-start.1) | collective-permute-done | bytes 1196064 | tf_op jit(solution)/shard_map/ppermute | solution.py:14
  588.7 2.3 fusion.36
  591.0 5.4 fusion.32
  596.5 1.5 select_maximum_fusion
  598.0 8.0 %fusion.10 = f32[3,262,2048]{2,1,0:T(8,128)S(1)} fusion(f32[3,268,2048]{2,1,0:T(8,128)S(1)} %select_maximum_fusion, f32[3,2048]{1,0:T(4,128)S(1)} %get-tuple-element.95, f32[3,2048]{1,0:T(4,128)S(1)} %get-tuple-element.96, f32[3,2048]{1,0:T(4,128)S(1)} %get-tuple-element.97, f32[3,2048]{1,0:T(4,128)S(1)} %copy-done.4, f32[3,2048]{1,0:T(4,128)S(1)} %get-tuple-element.99, ...), kind=kLoop, calls=%fused_computation.24 | loop fusion | flops 30584832 | bytes 51684900 | tf_op jit(solution)/shard_map/add | solution.py:44
  606.0 2.7 copy-done.1
  611.9 2.7 copy.84
  614.6 50.7 %all_to_all.23 = bf16[3,256,2048]{2,0,1:T(4,128)(2,1)S(1)} all-to-all(bf16[3,256,2048]{2,0,1:T(4,128)(2,1)S(1)} %copy.84), channel_id=1, replica_groups=mesh['seq'=8,'chan'=4] {'chan'}, dimensions={1} | all-to-all | bytes 6291456 | tf_op jit(solution)/shard_map/all_to_all | solution.py:141
  665.4 2.3 copy.85
  667.6 2.1 copy.94
  (71 shorter events, 14.3 us)
Async XLA Ops:
  2.7 6.6 copy-start.15
  2.7 7.4 %copy-start.8 = (f32[3,128,7]{1,2,0:T(8,128)S(1)}, f32[3,128,7]{1,2,0:T(8,128)}, u32[]{:S(2)}) copy-start(f32[3,128,7]{1,2,0:T(8,128)} %param.15) | copy-start | bytes 32260
  4.6 42.2 %all-to-all-start = ((bf16[4,3,64,2048]{3,2,1,0:T(8,128)(2,1)}), bf16[4,3,64,2048]{3,2,1,0:T(8,128)(2,1)}, u32[]{:S(2)}, u32[]{:S(2)}) async-start(bf16[4,3,64,2048]{3,2,1,0:T(8,128)(2,1)} %pad_maximum_fusion.1), calls=%async_computation | async-start | bytes 6291456 | tf_op jit(solution)/shard_map/all_to_all | solution.py:70
  9.4 47.4 %copy-start.5 = (s32[390]{0:T(512)}, s32[390]{0:T(512)S(1)}, u32[]{:S(2)}) copy-start(s32[390]{0:T(512)S(1)} %convert_reduce_fusion) | copy-start | bytes 4684
  10.5 46.4 %copy-start.7 = (f32[128,128]{1,0:T(8,128)S(1)}, f32[128,128]{1,0:T(8,128)}, u32[]{:S(2)}) copy-start(f32[128,128]{1,0:T(8,128)} %param.16) | copy-start | bytes 196612
  50.5 411.8 %collective-permute-start = (bf16[3,134,2048]{2,1,0:T(8,128)(2,1)}, bf16[3,134,2048]{2,1,0:T(8,128)(2,1)}, u32[]{:S(2)}, u32[]{:S(2)}) collective-permute-start(bf16[3,134,2048]{2,1,0:T(8,128)(2,1)} %slice.375), channel_id=1, source_target_pairs={{0,4},{4,8},{8,12},{12,16},{16,20},{20,24},{24,28},{1,5},{5,9},{9,... | collective-permute-start | bytes 4939784 | tf_op jit(solution)/shard_map/ppermute | solution.py:14
  462.3 92.6 %copy-start.3 = (f32[3,2048]{1,0:T(4,128)}, f32[3,2048]{1,0:T(4,128)S(1)}, u32[]{:S(2)}) copy-start(f32[3,2048]{1,0:T(4,128)S(1)} %get-tuple-element.98) | copy-start | bytes 73732
  507.4 3.6 copy-start
  548.6 3.1 slice-start
  548.6 5.9 copy-start.14
  548.6 6.3 copy-start.9
  548.6 6.3 copy-start.10
  548.6 6.3 copy-start.11
  548.6 6.3 copy-start.12
  548.6 6.3 copy-start.13
  554.4 4.8 copy-start.6
  557.9 30.8 %collective-permute-start.1 = (f32[146,2048]{1,0:T(8,128)}, f32[146,2048]{1,0:T(8,128)}, u32[]{:S(2)}, u32[]{:S(2)}) collective-permute-start(f32[146,2048]{1,0:T(8,128)} %pad_maximum_fusion.2), channel_id=1, source_target_pairs={{4,0},{8,4},{12,8},{16,12},{20,16},{24,20},{28,24},{5,1},{9,5},{13... | collective-permute-start | bytes 3588104 | tf_op jit(solution)/shard_map/ppermute | solution.py:14
  591.0 5.4 copy-start.2
  596.5 1.5 copy-start.4
  606.0 2.7 copy-start.1
